TPU v7x, 128 devices: a whole 4x4x4 slice. The times are simulated.
128 devices in a mesh: grp: 8 (over y_lo, z), tok: 16 (over y_hi, x, core).
Axes of the slice: x: 4, y: 4 (y_hi: 2, y_lo: 2; y = y_hi * 2 + y_lo), z: 4, core: 2. Of those that a mesh axis runs over, the one named last changes fastest.
Arguments:
- hidden: bfloat16 [8, 2048, 4608], P('grp', 'tok'), may hold values from -40 to 40
- input_gain: float32 [4608], replicated, may hold values from 0.25 to 1.75
- w_query: bfloat16 [4608, 4096], P(None, 'tok'), may hold values from -4 to 4
- w_key: bfloat16 [4608, 2048], P(None, 'tok'), may hold values from -4 to 4
- w_value: bfloat16 [4608, 2048], P(None, 'tok'), may hold values from -0.09375 to 0.09375
- w_out: bfloat16 [4096, 4608], P('tok'), may hold values from -0.09375 to 0.09375
- post_gain: float32 [4608], replicated, may hold values from 0.25 to 1.75
- cache_keys: bfloat16 [64, 256, 2048], P('grp', None, 'tok'), may hold values from -6 to 46
- cache_values: bfloat16 [64, 256, 2048], P('grp', None, 'tok'), may hold values from -6 to 6
- page_table: int32 [8, 8], replicated, may hold values from 0 to 63, as said below
- stretch_request: int32 [8, 8], P('grp'), may hold values from 0 to 2, never falling along the last dimension, each value on 1 to 4 neighbouring positions
- recompute_ids: int32 [8, 204], P('grp'), may hold values from 0 to 2047, as said below
- query_counts: int32 [8, 3], P('grp'), may hold values from 1 to 1024, 1844 in all within a row
Outputs:
- output: bfloat16 [8, 2048, 4608], P('grp', 'tok')
Inputs may be any that keep to these rules, and one draw needn't show every extreme that they name: `page_table`: row g lists the pages of group g's 8 stretch slots; page p is held by group p // 8; every page appears once, and the slots of a group take exactly one page from each group. `stretch_request`: each request of a group holds one or more consecutive slots, request numbers never fall along the slots, and one request holds (8 + 1) // 2 slots, none more. `recompute_ids`: each row holds 204 distinct cached tokens of the group (slot times 256 plus the token within the stretch) in rising order. `query_counts`: the counts of a group sum to 1844.
All inputs are finite; a program needn't handle non-finite values.
Results may differ from a plain program's by a relative error of at most 0.01.
Values may be sent and summed in bfloat16 or wider, within the bound.
A program may use at most 128 MiB of HBM per device.

v0:
```python
import math
import jax
import jax.numpy as jnp
from jax import lax
from jax.sharding import PartitionSpec as P

HEAD = 128
EPSILON = 1e-06
CAP_VALUE = 50.0
QUERY_SCALE = 1.0 / 12.0
ROPE_BASE = 10000.0


def rotate(tensor, positions):
    halfway = tensor.shape[-1] // 2
    ladder = jnp.arange(halfway).astype(jnp.float32)
    frequency = jnp.exp(ladder * (-2.0 * math.log(ROPE_BASE) / tensor.shape[-1]))
    angles = positions.astype(jnp.float32)[:, None] * frequency[None, :]
    cosine = jnp.cos(angles)[:, None, :]
    sine_values = jnp.sin(angles)[:, None, :]
    front_part = tensor[..., :halfway]
    back_part = tensor[..., halfway:]
    return jnp.concatenate(
        [
            front_part * cosine - back_part * sine_values,
            back_part * cosine + front_part * sine_values,
        ],
        axis=-1,
    )


def normalize(matrix, gain):
    widened = matrix.astype(jnp.float32)
    return widened * lax.rsqrt(jnp.mean(widened * widened, axis=-1, keepdims=True) + EPSILON) * gain


def request_layout(stretch_owner, counts_row, selected, stretch_len, new_rows):
    slot_total = stretch_owner.shape[0]
    requests = counts_row.shape[0]
    request_ids = jnp.arange(requests, dtype=jnp.int32)
    slot_ids = jnp.arange(slot_total, dtype=jnp.int32)
    belongs = (stretch_owner[:, None] == request_ids[None, :]).astype(jnp.int32)
    first_slot = jnp.sum((stretch_owner[None, :] < request_ids[:, None]).astype(jnp.int32), axis=1)
    stretch_count = jnp.sum(belongs, axis=0)
    offsets = (slot_ids - jnp.sum(belongs * first_slot[None, :], axis=1)) * stretch_len
    inner_ids = jnp.arange(stretch_len, dtype=jnp.int32)
    cache_pos = (offsets[:, None] + inner_ids[None, :]).reshape(-1)
    cache_req = jnp.broadcast_to(stretch_owner[:, None], (slot_total, stretch_len)).reshape(-1)
    cache_ids = jnp.arange(slot_total * stretch_len, dtype=jnp.int32)
    chosen = jnp.sum((selected[:, None] == cache_ids[None, :]).astype(jnp.int32), axis=0)
    cache_live = chosen == 0
    home_slot = ((selected // stretch_len)[:, None] == slot_ids[None, :]).astype(jnp.int32)
    select_req = jnp.sum(home_slot * stretch_owner[None, :], axis=1)
    select_pos = jnp.sum(home_slot * offsets[None, :], axis=1) + selected % stretch_len
    query_total = new_rows - selected.shape[0]
    query_ids = jnp.arange(query_total, dtype=jnp.int32)
    query_start = jnp.cumsum(counts_row) - counts_row
    query_req = jnp.sum((query_ids[:, None] >= query_start[None, 1:]).astype(jnp.int32), axis=1)
    mapping = (query_req[:, None] == request_ids[None, :]).astype(jnp.int32)
    query_pos = (
        jnp.sum(mapping * (stretch_count * stretch_len - query_start)[None, :], axis=1) + query_ids
    )
    row_req = jnp.concatenate([select_req, query_req])
    row_pos = jnp.concatenate([select_pos, query_pos])
    key_req = jnp.concatenate([cache_req, row_req])
    key_pos = jnp.concatenate([cache_pos, row_pos])
    key_live = jnp.concatenate([cache_live, jnp.ones((new_rows,), dtype=bool)])
    return (offsets, row_req, row_pos, key_req, key_pos, key_live)


def attend(queries, all_keys, all_values, row_req, row_pos, key_req, key_pos, key_live):
    scores = jnp.einsum("qcgd,kcd->cgqk", queries, all_keys, preferred_element_type=jnp.float32)
    capped = CAP_VALUE * jnp.tanh(scores * (QUERY_SCALE / CAP_VALUE))
    visible = (
        (key_req[None, :] == row_req[:, None])
        & (key_pos[None, :] <= row_pos[:, None])
        & key_live[None, :]
    ).astype(jnp.float32)
    weights = jnp.exp(capped) * visible[None, None]
    denominator = jnp.sum(weights, axis=-1)
    rounded = weights.astype(jnp.bfloat16)
    weighted = jnp.einsum("cgqk,kcd->qcgd", rounded, all_values, preferred_element_type=jnp.float32)
    result = weighted / jnp.transpose(denominator, (2, 0, 1))[..., None]
    return result.astype(jnp.bfloat16).reshape(queries.shape[0], -1)


def run_attention(query_rot, all_keys, all_values, rows_req, rows_pos, key_req, key_pos, key_live):
    total_rows = query_rot.shape[0]
    block_rows = min(512, total_rows)
    block_total = total_rows // block_rows

    def one_block(bundle):
        return attend(
            bundle[0], all_keys, all_values, bundle[1], bundle[2], key_req, key_pos, key_live
        )

    shaped = query_rot.reshape((block_total, block_rows) + query_rot.shape[1:])
    attended = lax.map(
        one_block,
        (
            shaped,
            rows_req.reshape(block_total, block_rows),
            rows_pos.reshape(block_total, block_rows),
        ),
    )
    return attended.reshape(total_rows, -1)


def on_device(
    hidden,
    input_gain,
    w_query,
    w_key,
    w_value,
    w_out,
    post_gain,
    cache_keys,
    cache_values,
    page_table,
    stretch_request,
    recompute_ids,
    query_counts,
):
    own_rows = hidden[0]
    row_count = own_rows.shape[0]
    tok_total = lax.axis_size("tok")
    new_rows = row_count * tok_total
    stretch_len = cache_keys.shape[1]
    key_heads = w_key.shape[1] // HEAD
    query_heads = w_query.shape[1] // HEAD
    group_size = query_heads // key_heads
    query_cols = w_query.shape[1]
    key_cols = w_key.shape[1]
    normed_own = normalize(own_rows, input_gain).astype(jnp.bfloat16)
    offsets, row_req, row_pos, key_req, key_pos, key_live = request_layout(
        stretch_request[0], query_counts[0], recompute_ids[0], stretch_len, new_rows
    )
    group_index = lax.axis_index("grp")
    my_pages = lax.dynamic_index_in_dim(page_table, group_index, 0, keepdims=False)
    sections = (
        lax.all_gather(cache_keys, "grp", axis=0, tiled=True),
        lax.all_gather(cache_values, "grp", axis=0, tiled=True),
    )
    section_rows = sections[0].shape[0]
    hits = (my_pages[:, None] == jnp.arange(section_rows, dtype=jnp.int32)[None, :]).astype(
        jnp.bfloat16
    )
    picked_keys = jnp.einsum("cp,pkh->ckh", hits, sections[0], preferred_element_type=jnp.float32)
    picked_values = jnp.einsum("cp,pkh->ckh", hits, sections[1], preferred_element_type=jnp.float32)
    page_keys = picked_keys.astype(jnp.bfloat16)
    page_values = picked_values.astype(jnp.bfloat16)
    slot_total = page_keys.shape[0]
    shifts = jnp.broadcast_to(offsets[:, None], (slot_total, stretch_len)).reshape(-1)
    segment = lax.all_gather(normed_own, "tok", axis=0, tiled=True)
    joined = jnp.concatenate(
        [
            jnp.dot(segment, w_query, preferred_element_type=jnp.float32),
            jnp.dot(segment, w_key, preferred_element_type=jnp.float32),
            jnp.dot(segment, w_value, preferred_element_type=jnp.float32),
        ],
        axis=1,
    )
    cached_k = rotate(
        page_keys.astype(jnp.float32).reshape(slot_total * stretch_len, key_heads, HEAD), shifts
    ).astype(jnp.bfloat16)
    cached_v = page_values.reshape(slot_total * stretch_len, key_heads, HEAD)
    query_rot = rotate(joined[:, :query_cols].reshape(new_rows, query_heads, HEAD), row_pos).astype(
        jnp.bfloat16
    )
    query_rot = query_rot.reshape(new_rows, key_heads, group_size, HEAD)
    key_rot = rotate(
        joined[:, query_cols : query_cols + key_cols].reshape(new_rows, key_heads, HEAD), row_pos
    ).astype(jnp.bfloat16)
    value_new = (
        joined[:, query_cols + key_cols :].astype(jnp.bfloat16).reshape(new_rows, key_heads, HEAD)
    )
    all_keys = jnp.concatenate([cached_k, key_rot], axis=0)
    all_values = jnp.concatenate([cached_v, value_new], axis=0)
    attended = run_attention(
        query_rot, all_keys, all_values, row_req, row_pos, key_req, key_pos, key_live
    )
    summed = lax.psum_scatter(
        jnp.dot(attended, w_out, preferred_element_type=jnp.float32).astype(jnp.bfloat16),
        "tok",
        scatter_dimension=0,
        tiled=True,
    ).astype(jnp.float32)
    result = own_rows.astype(jnp.float32) + normalize(summed, post_gain)
    return result.astype(jnp.bfloat16)[None]


def solution(mesh):
    return jax.shard_map(
        on_device,
        mesh=mesh,
        in_specs=(
            P("grp", "tok", None),
            P(),
            P(None, "tok"),
            P(None, "tok"),
            P(None, "tok"),
            P("tok", None),
            P(),
            P("grp", None, "tok"),
            P("grp", None, "tok"),
            P(),
            P("grp", None),
            P("grp", None),
            P("grp", None),
        ),
        out_specs=P("grp", "tok", None),
        check_vma=False,
    )
```

profile of v0, /device:TPU:1, one launch (start us, length us, event | category | flops | bytes accessed | tf_op | source)
XLA Modules:
  0.0 586.5 jit_solution(13476773845455432164)
XLA Ops:
  16.3 2.8 multiply_cosine_fusion.2
  19.1 51.7 %all-gather.6.cloned.1.call-done = bf16[64,256,128]{2,0,1:T(8,128)(2,1)} async-done(((bf16[8,256,128]{2,0,1:T(8,128)(2,1)}), bf16[64,256,128]{2,0,1:T(8,128)(2,1)}) %all-gather.6.cloned.1.call-update) | async-done | bytes 4194320 | tf_op jit(solution)/shard_map/all_gather | solution.py:141
  70.8 2.9 fusion.33
  78.7 54.7 %all-gather.8.cloned.1.call-done = bf16[64,256,128]{2,0,1:T(8,128)(2,1)} async-done(((bf16[8,256,128]{2,0,1:T(8,128)(2,1)}), bf16[64,256,128]{2,0,1:T(8,128)(2,1)}) %all-gather.8.cloned.1.call-update) | async-done | bytes 4194320 | tf_op jit(solution)/shard_map/all_gather | solution.py:142
  133.5 2.9 convolution_convert_fusion.2
  137.2 121.5 %all-gather.4.cloned.1.call-done = bf16[2048,4608]{1,0:T(8,128)(2,1)} async-done(((bf16[128,4608]{1,0:T(8,128)(2,1)}), bf16[2048,4608]{1,0:T(8,128)(2,1)}) %all-gather.4.cloned.1.call-update) | async-done | bytes 18874384 | tf_op jit(solution)/shard_map/all_gather | solution.py:154
  258.7 10.4 %convolution_bitcast_fusion = f32[2048,1,128]{0,2,1:T(8,128)S(1)} fusion(bf16[2048,4608]{1,0:T(8,128)(2,1)} %all-gather.4.cloned.1.call-done, bf16[4608,128]{1,0:T(8,128)(2,1)} %param.18), kind=kOutput, calls=%fused_computation.26 | convolution fusion | flops 2415919104 | bytes 21102592 | tf_op jit(solution)/shard_map/dot_general | solution.py:158
  269.2 5.2 fusion.48
  277.1 9.8 %fusion.63 = f32[2048,256]{0,1:T(8,128)S(1)} fusion(bf16[2048,4608]{1,0:T(8,128)(2,1)} %all-gather.4.cloned.1.call-done, bf16[4608,256]{1,0:T(8,128)(2,1)} %param.17), kind=kOutput, calls=%fused_computation.111 | convolution fusion | flops 4831838208 | bytes 23330816 | tf_op jit(solution)/shard_map/dot_general | solution.py:157
  292.7 2.8 pad_maximum_fusion
  295.5 2.6 copy.34
  298.2 9.4 %fusion.32 = bf16[2048,1,128]{2,0,1:T(8,128)(2,1)S(1)} fusion(bf16[2048,4608]{1,0:T(8,128)(2,1)} %all-gather.4.cloned.1.call-done, bf16[4608,128]{1,0:T(8,128)(2,1)} %param.19), kind=kOutput, calls=%fused_computation.34 | convolution fusion | flops 2416181248 | bytes 20578304 | tf_op jit(solution)/shard_map/dot_general | solution.py:159
  310.9 98.5 %while.10 = (s32[]{:T(128)}, bf16[4,512,256]{2,1,0:T(8,128)(2,1)}, bf16[4,512,1,2,128]{4,1,3,2,0:T(8,128)(2,1)}, bf16[4096,1,128]{2,0,1:T(8,128)(2,1)S(1)}, s32[...) while((s32[]{:T(128)}, bf16[4,512,256]{2,1,0:T(8,128)(2,1)}, ...), condition=%wide.region_12.13_spmd, body=%wide.region_10.12_spmd.sunk | while | flops 2191784960 | bytes 66643084 | solution.py:98
  312.7 9.9 %fusion.80 = (f32[2,512]{1,0:T(2,128)S(1)}, f32[512,2,4096]{2,0,1:T(8,128)}) fusion(f32[512,4096]{1,0:T(8,128)S(1)} %and_convert_fusion.2, bf16[4096,1,128]{2,0,1:T(8,128)(2,1)S(1)} %get-tuple-element.226, bf16[4,512,1,2,128]{4,1,3,2,0:T(8,128)(2,1)} %get-tuple-element.225, s32[]{:T(128)} %get-tuple-element.212), kind=kOutput, calls=%fused_computation.1.clone.1 | convolution fusion | flops 1090518016 | bytes 26481152 | tf_op jit(solution)/shard_map/while/body/eval_jaxpr/qcgd,kcd->cgqk/dot_general | solution.py:72
  322.6 9.4 %fusion.81 = bf16[512,1,2,128]{0,3,2,1:T(8,128)(2,1)} fusion(bf16[4096,1,128]{0,2,1:T(8,128)(2,1)S(1)} %copy-done.1, f32[512,2,4096]{2,0,1:T(8,128)} %get-tuple-element.199, f32[512,4096]{1,0:T(8,128)S(1)} %and_convert_fusion.2, f32[512,2]{0,1:T(2,128)S(1)} %bitcast.153), kind=kOutput, calls=%fused_computation.11.clone.1 | convolution fusion | flops 1090781184 | bytes 26480640 | tf_op jit(solution)/shard_map/while/body/eval_jaxpr/cgqk,kcd->qcgd/dot_general | solution.py:82
  337.4 9.9 %fusion.80 = (f32[2,512]{1,0:T(2,128)S(1)}, f32[512,2,4096]{2,0,1:T(8,128)}) fusion(f32[512,4096]{1,0:T(8,128)S(1)} %and_convert_fusion.2, bf16[4096,1,128]{2,0,1:T(8,128)(2,1)S(1)} %get-tuple-element.226, bf16[4,512,1,2,128]{4,1,3,2,0:T(8,128)(2,1)} %get-tuple-element.225, s32[]{:T(128)} %get-tuple-element.212), kind=kOutput, calls=%fused_computation.1.clone.1 | convolution fusion | flops 1090518016 | bytes 26481152 | tf_op jit(solution)/shard_map/while/body/eval_jaxpr/qcgd,kcd->cgqk/dot_general | solution.py:72
  347.3 9.4 %fusion.81 = bf16[512,1,2,128]{0,3,2,1:T(8,128)(2,1)} fusion(bf16[4096,1,128]{0,2,1:T(8,128)(2,1)S(1)} %copy-done.1, f32[512,2,4096]{2,0,1:T(8,128)} %get-tuple-element.199, f32[512,4096]{1,0:T(8,128)S(1)} %and_convert_fusion.2, f32[512,2]{0,1:T(2,128)S(1)} %bitcast.153), kind=kOutput, calls=%fused_computation.11.clone.1 | convolution fusion | flops 1090781184 | bytes 26480640 | tf_op jit(solution)/shard_map/while/body/eval_jaxpr/cgqk,kcd->qcgd/dot_general | solution.py:82
  362.0 9.9 %fusion.80 = (f32[2,512]{1,0:T(2,128)S(1)}, f32[512,2,4096]{2,0,1:T(8,128)}) fusion(f32[512,4096]{1,0:T(8,128)S(1)} %and_convert_fusion.2, bf16[4096,1,128]{2,0,1:T(8,128)(2,1)S(1)} %get-tuple-element.226, bf16[4,512,1,2,128]{4,1,3,2,0:T(8,128)(2,1)} %get-tuple-element.225, s32[]{:T(128)} %get-tuple-element.212), kind=kOutput, calls=%fused_computation.1.clone.1 | convolution fusion | flops 1090518016 | bytes 26481152 | tf_op jit(solution)/shard_map/while/body/eval_jaxpr/qcgd,kcd->cgqk/dot_general | solution.py:72
  371.9 9.4 %fusion.81 = bf16[512,1,2,128]{0,3,2,1:T(8,128)(2,1)} fusion(bf16[4096,1,128]{0,2,1:T(8,128)(2,1)S(1)} %copy-done.1, f32[512,2,4096]{2,0,1:T(8,128)} %get-tuple-element.199, f32[512,4096]{1,0:T(8,128)S(1)} %and_convert_fusion.2, f32[512,2]{0,1:T(2,128)S(1)} %bitcast.153), kind=kOutput, calls=%fused_computation.11.clone.1 | convolution fusion | flops 1090781184 | bytes 26480640 | tf_op jit(solution)/shard_map/while/body/eval_jaxpr/cgqk,kcd->qcgd/dot_general | solution.py:82
  386.6 9.9 %fusion.80 = (f32[2,512]{1,0:T(2,128)S(1)}, f32[512,2,4096]{2,0,1:T(8,128)}) fusion(f32[512,4096]{1,0:T(8,128)S(1)} %and_convert_fusion.2, bf16[4096,1,128]{2,0,1:T(8,128)(2,1)S(1)} %get-tuple-element.226, bf16[4,512,1,2,128]{4,1,3,2,0:T(8,128)(2,1)} %get-tuple-element.225, s32[]{:T(128)} %get-tuple-element.212), kind=kOutput, calls=%fused_computation.1.clone.1 | convolution fusion | flops 1090518016 | bytes 26481152 | tf_op jit(solution)/shard_map/while/body/eval_jaxpr/qcgd,kcd->cgqk/dot_general | solution.py:72
  396.5 9.4 %fusion.81 = bf16[512,1,2,128]{0,3,2,1:T(8,128)(2,1)} fusion(bf16[4096,1,128]{0,2,1:T(8,128)(2,1)S(1)} %copy-done.1, f32[512,2,4096]{2,0,1:T(8,128)} %get-tuple-element.199, f32[512,4096]{1,0:T(8,128)S(1)} %and_convert_fusion.2, f32[512,2]{0,1:T(2,128)S(1)} %bitcast.153), kind=kOutput, calls=%fused_computation.11.clone.1 | convolution fusion | flops 1090781184 | bytes 26480640 | tf_op jit(solution)/shard_map/while/body/eval_jaxpr/cgqk,kcd->qcgd/dot_general | solution.py:82
  409.4 10.3 %convolution_convert_fusion = bf16[2048,4608]{1,0:T(8,128)(2,1)} fusion(bf16[2048,256]{1,0:T(8,128)(2,1)} %bitcast.152, bf16[256,4608]{1,0:T(8,128)(2,1)S(1)} %copy-done), kind=kOutput, calls=%fused_computation.20 | convolution fusion | flops 4841275392 | bytes 22282240 | tf_op jit(solution)/shard_map/dot_general | solution.py:183
  419.7 156.0 %reduce-scatter.2.cloned.1.call-done = bf16[128,4608]{1,0:T(8,128)(2,1)} async-done(((bf16[2048,4608]{1,0:T(8,128)(2,1)}), bf16[128,4608]{1,0:T(8,128)(2,1)}) %reduce-scatter.2.cloned.1.call-update) | async-done | bytes 1179664 | tf_op jit(solution)/shard_map/reduce_scatter | solution.py:182
  577.2 2.8 fusion.34
  (100 shorter events, 50.1 us)
Async XLA Ops:
  6.5 402.8 %copy-start = (bf16[256,4608]{1,0:T(8,128)(2,1)S(1)}, bf16[256,4608]{1,0:T(8,128)(2,1)}, u32[]{:S(2)}) copy-start(bf16[256,4608]{1,0:T(8,128)(2,1)} %param.20) | copy-start | bytes 7077892
  6.5 4.8 copy-start.2
  6.5 64.3 %all-gather.6.cloned.1.call-start = ((), (), s32[]{:S(2)}) async-start(), calls=%async_computation.2 | async-start | bytes 4718592 | tf_op jit(solution)/shard_map/all_gather | solution.py:141
  9.0 124.5 %all-gather.8.cloned.1.call-start = ((), (), s32[]{:S(2)}) async-start(), calls=%async_computation.3 | async-start | bytes 4718592 | tf_op jit(solution)/shard_map/all_gather | solution.py:142
  11.2 2.6 copy-start.9
  11.2 2.9 copy-start.8
  11.3 3.5 copy-start.7
  11.3 247.5 %all-gather.4.cloned.1.call-start = ((), (), s32[]{:S(2)}) async-start(), calls=%async_computation.1 | async-start | bytes 20054016 | tf_op jit(solution)/shard_map/all_gather | solution.py:154
  13.8 561.9 %reduce-scatter.2.cloned.1.call-start = ((), (), s32[]{:S(2)}) async-start(), calls=%async_computation.4 | async-start | bytes 20054016 | tf_op jit(solution)/shard_map/reduce_scatter | solution.py:182
  277.1 9.8 %copy-start.5 = (f32[2048,64]{0,1:T(8,128)S(1)}, f32[2048,64]{0,1:T(8,128)}, u32[]{:S(2)}) copy-start(f32[2048,64]{0,1:T(8,128)} %get-tuple-element.126) | copy-start | bytes 1572868
  277.1 9.8 %copy-start.6 = (f32[2048,64]{0,1:T(8,128)S(1)}, f32[2048,64]{0,1:T(8,128)}, u32[]{:S(2)}) copy-start(f32[2048,64]{0,1:T(8,128)} %get-tuple-element.127) | copy-start | bytes 1572868
  298.2 9.4 %copy-start.4 = (bf16[8,256,128]{2,1,0:T(8,128)(2,1)S(1)}, bf16[8,256,128]{2,1,0:T(8,128)(2,1)}, u32[]{:S(2)}) copy-start(bf16[8,256,128]{2,1,0:T(8,128)(2,1)} %copy.33) | copy-start | bytes 1572868
  312.7 9.9 %copy-start.1 = (bf16[4096,1,128]{0,2,1:T(8,128)(2,1)S(1)}, bf16[4096,1,128]{0,2,1:T(8,128)(2,1)}, u32[]{:S(2)}) copy-start(bf16[4096,1,128]{0,2,1:T(8,128)(2,1)} %get-tuple-element.232) | copy-start | bytes 3145732 | tf_op jit(solution)/shard_map/while
  337.3 9.9 %copy-start.1 = (bf16[4096,1,128]{0,2,1:T(8,128)(2,1)S(1)}, bf16[4096,1,128]{0,2,1:T(8,128)(2,1)}, u32[]{:S(2)}) copy-start(bf16[4096,1,128]{0,2,1:T(8,128)(2,1)} %get-tuple-element.232) | copy-start | bytes 3145732 | tf_op jit(solution)/shard_map/while
  362.0 9.9 %copy-start.1 = (bf16[4096,1,128]{0,2,1:T(8,128)(2,1)S(1)}, bf16[4096,1,128]{0,2,1:T(8,128)(2,1)}, u32[]{:S(2)}) copy-start(bf16[4096,1,128]{0,2,1:T(8,128)(2,1)} %get-tuple-element.232) | copy-start | bytes 3145732 | tf_op jit(solution)/shard_map/while
  386.6 9.9 %copy-start.1 = (bf16[4096,1,128]{0,2,1:T(8,128)(2,1)S(1)}, bf16[4096,1,128]{0,2,1:T(8,128)(2,1)}, u32[]{:S(2)}) copy-start(bf16[4096,1,128]{0,2,1:T(8,128)(2,1)} %get-tuple-element.232) | copy-start | bytes 3145732 | tf_op jit(solution)/shard_map/while
  419.6 157.6 %copy-start.3 = (bf16[1,128,4608]{2,1,0:T(8,128)(2,1)S(1)}, bf16[1,128,4608]{2,1,0:T(8,128)(2,1)}, u32[]{:S(2)}) copy-start(bf16[1,128,4608]{2,1,0:T(8,128)(2,1)} %param.15) | copy-start | bytes 3538948
Sparse Core Ops, SparseCore 0:
  9.1 61.7 all-gather.5
  72.4 61.0 all-gather.7
  135.9 122.8 all-gather.3
  419.8 155.7 reduce-scatter.1
where the time goes:
time: 588 us; the launch traced here: 587 us
  waiting for transfers between devices  384 us (65%)
  matrix products  123 us (21%)
  local copies, waits for them, and re-layouts  36.6 us (6%)
  other arithmetic  29.6 us (5%)
  between operations  13.4 us (2%)
    reduce_scatter x1, waiting for transfers between devices, on_device(): lax.psum_scatter(jnp.dot(attended, w_out, preferred_element_type=jnp.floa...  156 us
    all_gather x1, waiting for transfers between devices, on_device(): segment = lax.all_gather(normed_own, 'tok', axis=0, tiled=True)  122 us
    all_gather x1, waiting for transfers between devices, on_device(): lax.all_gather(cache_values, 'grp', axis=0, tiled=True)  54.7 us
    all_gather x1, waiting for transfers between devices, on_device(): lax.all_gather(cache_keys, 'grp', axis=0, tiled=True)  51.7 us
    dot_general x4, matrix products, attend(): jnp.einsum('qcgd,kcd->cgqk', queries, all_keys, preferred_element_type=jn...  39.7 us
    dot_general x4, matrix products, attend(): jnp.einsum('cgqk,kcd->qcgd', rounded, all_values, preferred_element_type=...  37.4 us
    dynamic_update_slice x8, local copies, waits for them, and re-layouts, run_attention(): lax.map(one_block, (shaped, rows_req.reshape(block_total, block_rows), ro...  13.9 us
  transfers between devices with their start and end apart: 4, of which 4 were waited for; matrix products, arithmetic and copies ran while one was open for 4% of the time, Pallas kernels for 0%

commit v1 on v0

--- a/solution.py
+++ b/solution.py
@@ -151,7 +151,9 @@
     page_values = picked_values.astype(jnp.bfloat16)
     slot_total = page_keys.shape[0]
     shifts = jnp.broadcast_to(offsets[:, None], (slot_total, stretch_len)).reshape(-1)
-    segment = lax.all_gather(normed_own, "tok", axis=0, tiled=True)
+    segment = jnp.concatenate(
+        lax.all_to_all(jnp.stack([normed_own] * lax.axis_size("tok")), "tok", 0, 0), axis=0
+    )
     joined = jnp.concatenate(
         [
             jnp.dot(segment, w_query, preferred_element_type=jnp.float32),

time: 588 us -> 669 us (1.14)
  waiting for transfers between devices: 384 us -> 449 us
  starting transfers between devices: 0.13 us -> 8.7 us
    all_gather x1, waiting for transfers between devices: 51.7 us -> 227 us  [on_device(): lax.all_gather(cache_keys, 'grp', axis=0, tiled=True)]
    all_gather x1 -> x0, waiting for transfers between devices: 122 us -> none  [on_device(): segment = lax.all_gather(normed_own, 'tok', axis=0, tiled=True)]
    all_to_all x0 -> x1, starting transfers between devices: none -> 8.58 us  [on_device(): lax.all_to_all(jnp.stack([normed_own] * lax.axis_size('tok')), 'tok', 0, 0)]
    another operation x0 -> x1, local copies, waits for them, and re-layouts: none -> 6.82 us  [on_device(): jnp.stack([normed_own] * lax.axis_size('tok'))]
  transfers between devices with their start and end apart: 4 -> 4, of which waited for: 4 -> 3; matrix products, arithmetic and copies ran while one was open for 4% -> 4% of each run, Pallas kernels for 0% -> 0%
where the time goes in v1:
time: 669 us; the launch traced here: 668 us
  waiting for transfers between devices  449 us (67%)
  matrix products  123 us (18%)
  local copies, waits for them, and re-layouts  42.9 us (6%)
  other arithmetic  30.7 us (5%)
  between operations  13.4 us (2%)
  starting transfers between devices  8.7 us (1%)
    all_gather x1, waiting for transfers between devices, on_device(): lax.all_gather(cache_keys, 'grp', axis=0, tiled=True)  227 us
    reduce_scatter x1, waiting for transfers between devices, on_device(): lax.psum_scatter(jnp.dot(attended, w_out, preferred_element_type=jnp.floa...  161 us
    all_gather x1, waiting for transfers between devices, on_device(): lax.all_gather(cache_values, 'grp', axis=0, tiled=True)  60.2 us
    dot_general x4, matrix products, attend(): jnp.einsum('qcgd,kcd->cgqk', queries, all_keys, preferred_element_type=jn...  39.6 us
    dot_general x4, matrix products, attend(): jnp.einsum('cgqk,kcd->qcgd', rounded, all_values, preferred_element_type=...  37.5 us
    dynamic_update_slice x8, local copies, waits for them, and re-layouts, run_attention(): lax.map(one_block, (shaped, rows_req.reshape(block_total, block_rows), ro...  13.8 us
  transfers between devices with their start and end apart: 4, of which 3 were waited for; matrix products, arithmetic and copies ran while one was open for 4% of the time, Pallas kernels for 0%

profile of v1, /device:TPU:1, one launch (start us, length us, event | category | flops | bytes accessed | tf_op | source)
XLA Modules:
  0.0 667.6 jit_solution(11832511244407896080)
XLA Ops:
  9.9 6.8 %stack.5 = bf16[16,128,4608]{2,1,0:T(8,128)(2,1)} broadcast(bf16[128,4608]{1,0:T(8,128)(2,1)S(1)} %fusion.36), dimensions={1,2} | broadcast | bytes 20054016 | tf_op jit(solution)/shard_map/stack | solution.py:155
  16.7 8.6 %all-to-all-start = ((bf16[16,128,4608]{2,1,0:T(8,128)(2,1)}), bf16[16,128,4608]{2,1,0:T(8,128)(2,1)}, u32[]{:S(2)}, u32[]{:S(2)}) async-start(bf16[16,128,4608]{2,1,0:T(8,128)(2,1)} %stack.5), calls=%async_computation | async-start | bytes 37748736 | tf_op jit(solution)/shard_map/all_to_all | solution.py:155
  27.9 4.3 copy.45
  37.5 227.3 %all-gather.3.cloned.1.call-done = bf16[64,256,128]{2,0,1:T(8,128)(2,1)} async-done(((bf16[8,256,128]{2,0,1:T(8,128)(2,1)}), bf16[64,256,128]{2,0,1:T(8,128)(2,1)}) %all-gather.3.cloned.1.call-update) | async-done | bytes 4194320 | tf_op jit(solution)/shard_map/all_gather | solution.py:141
  264.7 2.9 fusion.35
  272.7 60.2 %all-gather.5.cloned.1.call-done = bf16[64,256,128]{2,0,1:T(8,128)(2,1)} async-done(((bf16[8,256,128]{2,0,1:T(8,128)(2,1)}), bf16[64,256,128]{2,0,1:T(8,128)(2,1)}) %all-gather.5.cloned.1.call-update) | async-done | bytes 4194320 | tf_op jit(solution)/shard_map/all_gather | solution.py:142
  332.9 2.9 convolution_convert_fusion.2
  336.7 9.8 %fusion.66 = f32[2048,2,128]{0,2,1:T(8,128)S(1)} fusion(bf16[2048,4608,1]{1,0,2:T(8,128)(2,1)} %bitcast.21, bf16[2,128,4608]{2,1,0:T(8,128)(2,1)} %bitcast.164), kind=kOutput, calls=%fused_computation.113 | convolution fusion | flops 4831838208 | bytes 23330816 | tf_op jit(solution)/shard_map/dot_general | solution.py:159
  352.3 10.4 %convolution_bitcast_fusion = f32[2048,1,128]{0,2,1:T(8,128)S(1)} fusion(bf16[2048,4608]{1,0:T(8,128)(2,1)} %bitcast.20, bf16[4608,128]{1,0:T(8,128)(2,1)} %param.18), kind=kOutput, calls=%fused_computation.27 | convolution fusion | flops 2415919104 | bytes 21102592 | tf_op jit(solution)/shard_map/dot_general | solution.py:160
  362.7 5.2 fusion.51
  370.6 9.4 %fusion.34 = bf16[2048,1,128]{2,0,1:T(8,128)(2,1)S(1)} fusion(bf16[2048,4608]{1,0:T(8,128)(2,1)} %bitcast.20, bf16[4608,128]{1,0:T(8,128)(2,1)} %param.19), kind=kOutput, calls=%fused_computation.35 | convolution fusion | flops 2416181248 | bytes 20578304 | tf_op jit(solution)/shard_map/dot_general | solution.py:161
  383.4 3.2 pad_maximum_fusion
  386.5 98.4 %while.10 = (s32[]{:T(128)}, bf16[4,512,256]{2,1,0:T(8,128)(2,1)}, bf16[4,512,1,2,128]{4,1,3,2,0:T(8,128)(2,1)}, bf16[4096,1,128]{2,0,1:T(8,128)(2,1)S(1)}, s32[...) while((s32[]{:T(128)}, bf16[4,512,256]{2,1,0:T(8,128)(2,1)}, ...), condition=%wide.region_12.13_spmd, body=%wide.region_10.12_spmd.sunk | while | flops 2191784960 | bytes 66642076 | solution.py:98
  388.4 9.9 %fusion.83 = (f32[2,512]{1,0:T(2,128)S(1)}, f32[512,2,4096]{2,0,1:T(8,128)}) fusion(f32[512,4096]{1,0:T(8,128)S(1)} %and_convert_fusion.2, bf16[4096,1,128]{2,0,1:T(8,128)(2,1)S(1)} %get-tuple-element.226, bf16[4,512,1,2,128]{4,1,3,2,0:T(8,128)(2,1)} %get-tuple-element.225, s32[]{:T(128)S(6)} %copy.58), kind=kOutput, calls=%fused_computation.1.clone.1 | convolution fusion | flops 1090518016 | bytes 26480644 | tf_op jit(solution)/shard_map/while/body/eval_jaxpr/qcgd,kcd->cgqk/dot_general | solution.py:72
  398.3 9.4 %fusion.84 = bf16[512,1,2,128]{0,3,2,1:T(8,128)(2,1)} fusion(bf16[4096,1,128]{0,2,1:T(8,128)(2,1)S(1)} %copy-done.1, f32[512,2,4096]{2,0,1:T(8,128)} %get-tuple-element.199, f32[512,4096]{1,0:T(8,128)S(1)} %and_convert_fusion.2, f32[512,2]{0,1:T(2,128)S(1)} %bitcast.167), kind=kOutput, calls=%fused_computation.11.clone.1 | convolution fusion | flops 1090781184 | bytes 26480640 | tf_op jit(solution)/shard_map/while/body/eval_jaxpr/cgqk,kcd->qcgd/dot_general | solution.py:82
  413.0 9.9 %fusion.83 = (f32[2,512]{1,0:T(2,128)S(1)}, f32[512,2,4096]{2,0,1:T(8,128)}) fusion(f32[512,4096]{1,0:T(8,128)S(1)} %and_convert_fusion.2, bf16[4096,1,128]{2,0,1:T(8,128)(2,1)S(1)} %get-tuple-element.226, bf16[4,512,1,2,128]{4,1,3,2,0:T(8,128)(2,1)} %get-tuple-element.225, s32[]{:T(128)S(6)} %copy.58), kind=kOutput, calls=%fused_computation.1.clone.1 | convolution fusion | flops 1090518016 | bytes 26480644 | tf_op jit(solution)/shard_map/while/body/eval_jaxpr/qcgd,kcd->cgqk/dot_general | solution.py:72
  422.9 9.4 %fusion.84 = bf16[512,1,2,128]{0,3,2,1:T(8,128)(2,1)} fusion(bf16[4096,1,128]{0,2,1:T(8,128)(2,1)S(1)} %copy-done.1, f32[512,2,4096]{2,0,1:T(8,128)} %get-tuple-element.199, f32[512,4096]{1,0:T(8,128)S(1)} %and_convert_fusion.2, f32[512,2]{0,1:T(2,128)S(1)} %bitcast.167), kind=kOutput, calls=%fused_computation.11.clone.1 | convolution fusion | flops 1090781184 | bytes 26480640 | tf_op jit(solution)/shard_map/while/body/eval_jaxpr/cgqk,kcd->qcgd/dot_general | solution.py:82
  437.6 9.9 %fusion.83 = (f32[2,512]{1,0:T(2,128)S(1)}, f32[512,2,4096]{2,0,1:T(8,128)}) fusion(f32[512,4096]{1,0:T(8,128)S(1)} %and_convert_fusion.2, bf16[4096,1,128]{2,0,1:T(8,128)(2,1)S(1)} %get-tuple-element.226, bf16[4,512,1,2,128]{4,1,3,2,0:T(8,128)(2,1)} %get-tuple-element.225, s32[]{:T(128)S(6)} %copy.58), kind=kOutput, calls=%fused_computation.1.clone.1 | convolution fusion | flops 1090518016 | bytes 26480644 | tf_op jit(solution)/shard_map/while/body/eval_jaxpr/qcgd,kcd->cgqk/dot_general | solution.py:72
  447.5 9.4 %fusion.84 = bf16[512,1,2,128]{0,3,2,1:T(8,128)(2,1)} fusion(bf16[4096,1,128]{0,2,1:T(8,128)(2,1)S(1)} %copy-done.1, f32[512,2,4096]{2,0,1:T(8,128)} %get-tuple-element.199, f32[512,4096]{1,0:T(8,128)S(1)} %and_convert_fusion.2, f32[512,2]{0,1:T(2,128)S(1)} %bitcast.167), kind=kOutput, calls=%fused_computation.11.clone.1 | convolution fusion | flops 1090781184 | bytes 26480640 | tf_op jit(solution)/shard_map/while/body/eval_jaxpr/cgqk,kcd->qcgd/dot_general | solution.py:82
  462.2 9.9 %fusion.83 = (f32[2,512]{1,0:T(2,128)S(1)}, f32[512,2,4096]{2,0,1:T(8,128)}) fusion(f32[512,4096]{1,0:T(8,128)S(1)} %and_convert_fusion.2, bf16[4096,1,128]{2,0,1:T(8,128)(2,1)S(1)} %get-tuple-element.226, bf16[4,512,1,2,128]{4,1,3,2,0:T(8,128)(2,1)} %get-tuple-element.225, s32[]{:T(128)S(6)} %copy.58), kind=kOutput, calls=%fused_computation.1.clone.1 | convolution fusion | flops 1090518016 | bytes 26480644 | tf_op jit(solution)/shard_map/while/body/eval_jaxpr/qcgd,kcd->cgqk/dot_general | solution.py:72
  472.1 9.4 %fusion.84 = bf16[512,1,2,128]{0,3,2,1:T(8,128)(2,1)} fusion(bf16[4096,1,128]{0,2,1:T(8,128)(2,1)S(1)} %copy-done.1, f32[512,2,4096]{2,0,1:T(8,128)} %get-tuple-element.199, f32[512,4096]{1,0:T(8,128)S(1)} %and_convert_fusion.2, f32[512,2]{0,1:T(2,128)S(1)} %bitcast.167), kind=kOutput, calls=%fused_computation.11.clone.1 | convolution fusion | flops 1090781184 | bytes 26480640 | tf_op jit(solution)/shard_map/while/body/eval_jaxpr/cgqk,kcd->qcgd/dot_general | solution.py:82
  484.9 10.3 %convolution_convert_fusion = bf16[2048,4608]{1,0:T(8,128)(2,1)} fusion(bf16[2048,256]{1,0:T(8,128)(2,1)} %bitcast.166, bf16[256,4608]{1,0:T(8,128)(2,1)S(1)} %copy-done), kind=kOutput, calls=%fused_computation.20 | convolution fusion | flops 4841275392 | bytes 22282240 | tf_op jit(solution)/shard_map/dot_general | solution.py:185
  495.2 161.5 %reduce-scatter.2.cloned.1.call-done = bf16[128,4608]{1,0:T(8,128)(2,1)} async-done(((bf16[2048,4608]{1,0:T(8,128)(2,1)}), bf16[128,4608]{1,0:T(8,128)(2,1)}) %reduce-scatter.2.cloned.1.call-update) | async-done | bytes 1179664 | tf_op jit(solution)/shard_map/reduce_scatter | solution.py:184
  658.3 2.8 fusion.37
  (104 shorter events, 51.5 us)
Async XLA Ops:
  6.5 478.4 %copy-start = (bf16[256,4608]{1,0:T(8,128)(2,1)S(1)}, bf16[256,4608]{1,0:T(8,128)(2,1)}, u32[]{:S(2)}) copy-start(bf16[256,4608]{1,0:T(8,128)(2,1)} %param.20) | copy-start | bytes 7077892
  16.7 8.6 %copy-start.6 = (bf16[8,256,128]{2,1,0:T(8,128)(2,1)S(1)}, bf16[8,256,128]{2,1,0:T(8,128)(2,1)}, u32[]{:S(2)}) copy-start(bf16[8,256,128]{2,1,0:T(8,128)(2,1)} %param.22) | copy-start | bytes 1572868
  16.7 9.8 %copy-start.7 = (bf16[8,256,128]{2,1,0:T(8,128)(2,1)S(1)}, bf16[8,256,128]{2,1,0:T(8,128)(2,1)}, u32[]{:S(2)}) copy-start(bf16[8,256,128]{2,1,0:T(8,128)(2,1)} %param.23) | copy-start | bytes 1572868
  16.7 320.0 %all-to-all-start = ((bf16[16,128,4608]{2,1,0:T(8,128)(2,1)}), bf16[16,128,4608]{2,1,0:T(8,128)(2,1)}, u32[]{:S(2)}, u32[]{:S(2)}) async-start(bf16[16,128,4608]{2,1,0:T(8,128)(2,1)} %stack.5), calls=%async_computation | async-start | bytes 37748736 | tf_op jit(solution)/shard_map/all_to_all | solution.py:155
  25.3 239.4 %all-gather.3.cloned.1.call-start = ((), (), s32[]{:S(2)}) async-start(), calls=%async_computation.2 | async-start | bytes 4718592 | tf_op jit(solution)/shard_map/all_gather | solution.py:141
  26.5 306.4 %all-gather.5.cloned.1.call-start = ((), (), s32[]{:S(2)}) async-start(), calls=%async_computation.3 | async-start | bytes 4718592 | tf_op jit(solution)/shard_map/all_gather | solution.py:142
  27.8 628.9 %reduce-scatter.2.cloned.1.call-start = ((), (), s32[]{:S(2)}) async-start(), calls=%async_computation.4 | async-start | bytes 20054016 | tf_op jit(solution)/shard_map/reduce_scatter | solution.py:184
  27.9 4.4 copy-start.10
  27.9 4.6 copy-start.9
  27.9 5.1 copy-start.8
  336.7 9.8 %copy-start.4 = (f32[2048,64]{0,1:T(8,128)S(1)}, f32[2048,64]{0,1:T(8,128)}, u32[]{:S(2)}) copy-start(f32[2048,64]{0,1:T(8,128)} %get-tuple-element.126) | copy-start | bytes 1572868
  336.7 9.8 %copy-start.5 = (f32[2048,64]{0,1:T(8,128)S(1)}, f32[2048,64]{0,1:T(8,128)}, u32[]{:S(2)}) copy-start(f32[2048,64]{0,1:T(8,128)} %get-tuple-element.127) | copy-start | bytes 1572868
  370.6 9.4 %copy-start.3 = (bf16[8,256,128]{2,1,0:T(8,128)(2,1)S(1)}, bf16[8,256,128]{2,1,0:T(8,128)(2,1)}, u32[]{:S(2)}) copy-start(bf16[8,256,128]{2,1,0:T(8,128)(2,1)} %copy.41) | copy-start | bytes 1572868
  388.4 9.9 %copy-start.1 = (bf16[4096,1,128]{0,2,1:T(8,128)(2,1)S(1)}, bf16[4096,1,128]{0,2,1:T(8,128)(2,1)}, u32[]{:S(2)}) copy-start(bf16[4096,1,128]{0,2,1:T(8,128)(2,1)} %get-tuple-element.232) | copy-start | bytes 3145732 | tf_op jit(solution)/shard_map/while
  413.0 9.9 %copy-start.1 = (bf16[4096,1,128]{0,2,1:T(8,128)(2,1)S(1)}, bf16[4096,1,128]{0,2,1:T(8,128)(2,1)}, u32[]{:S(2)}) copy-start(bf16[4096,1,128]{0,2,1:T(8,128)(2,1)} %get-tuple-element.232) | copy-start | bytes 3145732 | tf_op jit(solution)/shard_map/while
  437.6 9.9 %copy-start.1 = (bf16[4096,1,128]{0,2,1:T(8,128)(2,1)S(1)}, bf16[4096,1,128]{0,2,1:T(8,128)(2,1)}, u32[]{:S(2)}) copy-start(bf16[4096,1,128]{0,2,1:T(8,128)(2,1)} %get-tuple-element.232) | copy-start | bytes 3145732 | tf_op jit(solution)/shard_map/while
  462.1 9.9 %copy-start.1 = (bf16[4096,1,128]{0,2,1:T(8,128)(2,1)S(1)}, bf16[4096,1,128]{0,2,1:T(8,128)(2,1)}, u32[]{:S(2)}) copy-start(bf16[4096,1,128]{0,2,1:T(8,128)(2,1)} %get-tuple-element.232) | copy-start | bytes 3145732 | tf_op jit(solution)/shard_map/while
  495.2 163.1 %copy-start.2 = (bf16[1,128,4608]{2,1,0:T(8,128)(2,1)S(1)}, bf16[1,128,4608]{2,1,0:T(8,128)(2,1)}, u32[]{:S(2)}) copy-start(bf16[1,128,4608]{2,1,0:T(8,128)(2,1)} %param.15) | copy-start | bytes 3538948
Sparse Core Ops, SparseCore 0:
  27.7 236.9 all-gather.2
  266.3 66.5 all-gather.4
  495.3 161.3 reduce-scatter.1
